TPU v7x, 32 devices: a whole 2x2x4 slice. The times are simulated.
32 devices in a mesh: rep: 2 (over y), blk: 4 (over z), sect: 2 (over x), sub: 2 (over core).
Axes of the slice: x: 2, y: 2, z: 4, core: 2. Of those that a mesh axis runs over, the one named last changes fastest.
Arguments:
- query_latent: bfloat16 [64, 128, 512], P(('rep', 'blk')), parts along dimension 0, may hold values from -192 to 192
- query_rope: bfloat16 [64, 64, 128], P(('rep', 'blk')), parts along dimension 0, may hold values from -18 to 18
- cache_latent: bfloat16 [32, 256, 512], P(('rep', 'blk', 'sect', 'sub')), parts along dimension 0, may hold values from -16 to 16
- cache_rope: bfloat16 [32, 64, 256], P(('rep', 'blk', 'sect', 'sub')), parts along dimension 0, may hold values from -4.5 to 4.5
- lengths: int32 [32], P('rep'), parts along dimension 0, may hold values from 64 to 256, as said below
- positions: int32 [64], P(('rep', 'blk')), parts along dimension 0, may hold values from 2048 to 4095
- value_weight: bfloat16 [128, 512, 128], P(('sect', 'sub')), may hold values from -0.25 to 0.25
Outputs:
- attended: bfloat16 [64, 128, 128], P(('rep', 'blk'), ('sect', 'sub')), parts along dimension 0
There are 2 independent parts, one for each index of `rep`. A program takes and returns all parts, laid end to end along the dimension named above; an argument that names none is the same for every part. Nothing has to cross between parts.
Inputs may be any that keep to these rules, and one draw needn't show every extreme that they name: `lengths`: in every draw some block has all 256 slots valid.
All inputs are finite; a program needn't handle non-finite values.
Results may differ from a plain program's by a relative error of at most 0.0075.
Values may be sent and summed in bfloat16 or wider, within the bound.
A program may use at most 64 MiB of HBM per device.

v0:
```python
import math

import jax
import jax.numpy as jnp
from jax import lax
from jax.sharding import PartitionSpec as P

lowest_score = -1e30


def shifted(value, axis, steps):
    count = lax.axis_size(axis)
    pairs = [(source, (source + steps) % count) for source in range(count)]
    return lax.ppermute(value, axis, pairs)


def visible_mask(positions, length, root, token_count, head_count):
    offsets = lax.broadcasted_iota(jnp.int32, (1, token_count), 1)
    places = root * token_count + offsets
    visible = (offsets < length) & (places <= positions[:, None])
    query_count = positions.shape[0]
    return jnp.broadcast_to(visible[:, None, :], (query_count, head_count, token_count)).reshape(
        query_count * head_count, token_count
    )


def absorb_block(partials, latent_rows, rope_rows, block_latent, block_rope, visible, score_scale):
    running_max, running_sum, running_out = partials
    scores = lax.dot_general(
        latent_rows, block_latent, (((1,), (1,)), ((), ())), preferred_element_type=jnp.float32
    )
    scores = scores + jnp.dot(rope_rows, block_rope, preferred_element_type=jnp.float32)
    scores = jnp.where(visible, scores * score_scale, lowest_score)
    new_max = jnp.maximum(running_max, jnp.max(scores, axis=1))
    factor = jnp.exp(running_max - new_max)
    weights = jnp.where(visible, jnp.exp(scores - new_max[:, None]), 0.0)
    running_sum = running_sum * factor + jnp.sum(weights, axis=1)
    running_out = running_out * factor[:, None] + jnp.dot(
        weights.astype(jnp.bfloat16), block_latent, preferred_element_type=jnp.float32
    )
    return (new_max, running_sum, running_out)


def shards(query_latent, query_rope, cache_latent, cache_rope, lengths, positions, value_weight):
    query_count, head_count, latent_width = query_latent.shape
    token_count = cache_latent.shape[1]
    score_scale = 1.0 / math.sqrt(latent_width + query_rope.shape[1])
    latent_rows = query_latent.reshape(query_count * head_count, latent_width)
    rope_rows = jnp.transpose(query_rope, (0, 2, 1)).reshape(
        query_count * head_count, query_rope.shape[1]
    )
    blk_count = lax.axis_size("blk")
    blk_place = lax.axis_index("blk")
    group_place = lax.axis_index(("sect", "sub"))
    group_size = lax.axis_size(("sect", "sub"))
    block_ids = lax.broadcasted_iota(jnp.int32, lengths.shape, 0)

    def absorb(partials, cache_block, offset_steps):
        root = (blk_place - offset_steps) % blk_count * group_size + group_place
        length = jnp.sum(jnp.where(block_ids == root, lengths, 0))
        visible = visible_mask(positions, length, root, token_count, head_count)
        return absorb_block(
            partials, latent_rows, rope_rows, cache_block[0], cache_block[1], visible, score_scale
        )

    rows_total = query_count * head_count
    partials = (
        jnp.full((rows_total,), lowest_score, jnp.float32),
        jnp.zeros((rows_total,), jnp.float32),
        jnp.zeros((rows_total, latent_width), jnp.float32),
    )
    own_block = (cache_latent[0], cache_rope[0])

    def advance(index_step, carry):
        cache_block, inner_partials = carry
        inner_partials = absorb(inner_partials, cache_block, index_step)
        cache_block = shifted((cache_block[0], cache_block[1]), "blk", 1)
        return (cache_block, inner_partials)

    last_block, partials = lax.fori_loop(0, blk_count - 1, advance, (own_block, partials))
    partials = absorb(partials, last_block, blk_count - 1)
    running_max = partials[0].reshape(query_count, head_count)
    running_sum = partials[1].reshape(query_count, head_count)
    running_out = partials[2].reshape(query_count, head_count, latent_width)
    parts_max, parts_sum, parts_out = (
        lax.all_to_all(running_max[None], ("sect", "sub"), split_axis=2, concat_axis=0, tiled=True),
        lax.all_to_all(running_sum[None], ("sect", "sub"), split_axis=2, concat_axis=0, tiled=True),
        lax.all_to_all(running_out[None], ("sect", "sub"), split_axis=2, concat_axis=0, tiled=True),
    )
    overall = jnp.max(parts_max, axis=0)
    factor = jnp.exp(parts_max - overall[None])
    numerator = jnp.sum(parts_out * factor[:, :, :, None], axis=0)
    denominator = jnp.sum(parts_sum * factor, axis=0)
    latent = (numerator / denominator[:, :, None]).astype(jnp.bfloat16)
    return jnp.einsum(
        "qhl,hld->qhd", latent, value_weight, preferred_element_type=jnp.float32
    ).astype(jnp.bfloat16)


def solution(mesh):
    placed = (
        P(("rep", "blk"), None, None),
        P(("rep", "blk"), None, None),
        P(("rep", "blk", "sect", "sub"), None, None),
        P(("rep", "blk", "sect", "sub"), None, None),
        P("rep"),
        P(("rep", "blk")),
        P(("sect", "sub"), None, None),
    )
    return jax.shard_map(
        shards,
        mesh=mesh,
        in_specs=placed,
        out_specs=P(("rep", "blk"), ("sect", "sub"), None),
        check_vma=False,
    )
```

profile of v0, /device:TPU:0, one launch (start us, length us, event | category | flops | bytes accessed | tf_op | source)
XLA Modules:
  0.0 91.6 jit_solution(1486528687058373556)
XLA Ops:
  0.0 0.9 %copy.82 = bf16[1,256,512]{2,1,0:T(8,128)(2,1)S(1)} copy(bf16[1,256,512]{2,1,0:T(8,128)(2,1)} %param.11) | data formatting | bytes 524288
  1.0 0.8 copy.83
  1.7 1.3 %fusion.26 = s32[]{:T(128)} fusion(s32[16]{0:T(128)} %param.13, s32[]{:T(128)S(6)} %add.124), kind=kLoop, calls=%fused_computation.48 | loop fusion | flops 47 | bytes 72 | tf_op jit(solution)/shard_map/reduce_sum | solution.py:60
  3.0 0.6 iota_compare_fusion.1
  3.7 0.7 compare_and_fusion.1
  4.6 1.1 %copy.27 = bf16[8,128,64]{2,1,0:T(8,128)(2,1)S(1)} copy(bf16[8,128,64]{1,2,0:T(8,128)(2,1)} %bitcast.107) | data formatting | bytes 262144 | tf_op jit(solution)/shard_map/transpose | solution.py:49
  5.7 31.4 %while.24 = (s32[]{:T(128)}, bf16[256,512]{1,0:T(8,128)(2,1)S(1)}, bf16[64,256]{1,0:T(8,128)(2,1)S(1)}, f32[1024]{0:T(1024)S(1)}, f32[1024]{0:T(1024)S(1)}, /*in...) while((s32[]{:T(128)}, bf16[256,512]{1,0:T(8,128)(2,1)S(1)}, ...), condition=%wide.region_4.5_spmd.clone, body=%wide.region_0.4_spmd.clone.sunk | while | flops 574629376 | bytes 14068742 | solution.py:80
  5.7 3.1 %collective-permute-start = (bf16[256,512]{1,0:T(8,128)(2,1)S(1)}, bf16[256,512]{1,0:T(8,128)(2,1)S(1)}, u32[]{:S(2)}, u32[]{:S(2)}) collective-permute-start(bf16[256,512]{1,0:T(8,128)(2,1)S(1)} %copy.69), channel_id=1, source_target_pairs={{0,4},{4,8},{8,12},{12,0},{1,5},{5,9},{9,13},{13,1},{2,6},{6,10},{... | collective-permute-start | bytes 786440 | tf_op jit(solution)/shard_map/while/body/eval_jaxpr/ppermute | solution.py:14
  8.8 1.6 %collective-permute-start.1 = (bf16[64,256]{1,0:T(8,128)(2,1)S(1)}, bf16[64,256]{1,0:T(8,128)(2,1)S(1)}, u32[]{:S(2)}, u32[]{:S(2)}) collective-permute-start(bf16[64,256]{1,0:T(8,128)(2,1)S(1)} %copy.70), channel_id=1, source_target_pairs={{0,4},{4,8},{8,12},{12,0},{1,5},{5,9},{9,13},{13,1},{2,6},{6,10},{... | collective-permute-start | bytes 98312 | tf_op jit(solution)/shard_map/while/body/eval_jaxpr/ppermute | solution.py:14
  10.4 1.3 %fusion.63 = s32[]{:T(128)} fusion(s32[16]{0:T(128)} %get-tuple-element.521, s32[]{:T(128)S(6)} %add.175), kind=kLoop, calls=%fused_computation.19.clone.1 | loop fusion | flops 47 | bytes 72 | tf_op jit(solution)/shard_map/while/body/eval_jaxpr/reduce_sum | solution.py:60
  11.7 0.6 iota_compare_fusion.3
  12.4 0.7 compare_and_fusion.3
  13.3 1.7 %fusion.62 = f32[1024,256]{0,1:T(8,128)S(1)} fusion(bf16[1024,512]{1,0:T(8,128)(2,1)} %get-tuple-element.523, bf16[256,512]{1,0:T(8,128)(2,1)S(1)} %copy.69), kind=kOutput, calls=%fused_computation.52.clone.1 | convolution fusion | flops 268435456 | bytes 2359296 | tf_op jit(solution)/shard_map/while/body/eval_jaxpr/dot_general | solution.py:29
  16.0 0.7 fusion.67
  16.8 1.1 %collective-permute-done.1 = bf16[64,256]{1,0:T(8,128)(2,1)S(1)} collective-permute-done((bf16[64,256]{1,0:T(8,128)(2,1)S(1)}, bf16[64,256]{1,0:T(8,128)(2,1)S(1)}, u32[]{:S(2)}, u32[]{:S(2)}) %collective-permute-start.1) | collective-permute-done | bytes 32800 | tf_op jit(solution)/shard_map/while/body/eval_jaxpr/ppermute | solution.py:14
  17.9 0.6 collective-permute-start
  18.5 0.7 collective-permute-start.1
  19.2 1.3 %fusion.63 = s32[]{:T(128)} fusion(s32[16]{0:T(128)} %get-tuple-element.521, s32[]{:T(128)S(6)} %add.175), kind=kLoop, calls=%fused_computation.19.clone.1 | loop fusion | flops 47 | bytes 72 | tf_op jit(solution)/shard_map/while/body/eval_jaxpr/reduce_sum | solution.py:60
  20.5 0.6 iota_compare_fusion.3
  21.2 0.7 compare_and_fusion.3
  22.1 1.7 %fusion.62 = f32[1024,256]{0,1:T(8,128)S(1)} fusion(bf16[1024,512]{1,0:T(8,128)(2,1)} %get-tuple-element.523, bf16[256,512]{1,0:T(8,128)(2,1)S(1)} %copy.69), kind=kOutput, calls=%fused_computation.52.clone.1 | convolution fusion | flops 268435456 | bytes 2359296 | tf_op jit(solution)/shard_map/while/body/eval_jaxpr/dot_general | solution.py:29
  24.9 0.7 fusion.67
  25.6 2.3 %collective-permute-done.1 = bf16[64,256]{1,0:T(8,128)(2,1)S(1)} collective-permute-done((bf16[64,256]{1,0:T(8,128)(2,1)S(1)}, bf16[64,256]{1,0:T(8,128)(2,1)S(1)}, u32[]{:S(2)}, u32[]{:S(2)}) %collective-permute-start.1) | collective-permute-done | bytes 32800 | tf_op jit(solution)/shard_map/while/body/eval_jaxpr/ppermute | solution.py:14
  28.0 1.4 %collective-permute-start.1 = (bf16[64,256]{1,0:T(8,128)(2,1)S(1)}, bf16[64,256]{1,0:T(8,128)(2,1)S(1)}, u32[]{:S(2)}, u32[]{:S(2)}) collective-permute-start(bf16[64,256]{1,0:T(8,128)(2,1)S(1)} %copy.70), channel_id=1, source_target_pairs={{0,4},{4,8},{8,12},{12,0},{1,5},{5,9},{9,13},{13,1},{2,6},{6,10},{... | collective-permute-start | bytes 98312 | tf_op jit(solution)/shard_map/while/body/eval_jaxpr/ppermute | solution.py:14
  29.4 1.3 %fusion.63 = s32[]{:T(128)} fusion(s32[16]{0:T(128)} %get-tuple-element.521, s32[]{:T(128)S(6)} %add.175), kind=kLoop, calls=%fused_computation.19.clone.1 | loop fusion | flops 47 | bytes 72 | tf_op jit(solution)/shard_map/while/body/eval_jaxpr/reduce_sum | solution.py:60
  30.7 0.6 iota_compare_fusion.3
  31.4 0.7 compare_and_fusion.3
  32.3 1.7 %fusion.62 = f32[1024,256]{0,1:T(8,128)S(1)} fusion(bf16[1024,512]{1,0:T(8,128)(2,1)} %get-tuple-element.523, bf16[256,512]{1,0:T(8,128)(2,1)S(1)} %copy.69), kind=kOutput, calls=%fused_computation.52.clone.1 | convolution fusion | flops 268435456 | bytes 2359296 | tf_op jit(solution)/shard_map/while/body/eval_jaxpr/dot_general | solution.py:29
  35.0 0.7 fusion.67
  35.8 1.3 %collective-permute-done.1 = bf16[64,256]{1,0:T(8,128)(2,1)S(1)} collective-permute-done((bf16[64,256]{1,0:T(8,128)(2,1)S(1)}, bf16[64,256]{1,0:T(8,128)(2,1)S(1)}, u32[]{:S(2)}, u32[]{:S(2)}) %collective-permute-start.1) | collective-permute-done | bytes 32800 | tf_op jit(solution)/shard_map/while/body/eval_jaxpr/ppermute | solution.py:14
  37.1 1.7 %fusion.32 = f32[256,1024]{1,0:T(8,128)S(1)} fusion(bf16[256,512]{1,0:T(8,128)(2,1)S(1)} %get-tuple-element.320, bf16[1024,512]{1,0:T(8,128)(2,1)} %get-tuple-element.531), kind=kOutput, calls=%fused_computation.53 | convolution fusion | flops 268435456 | bytes 2359296 | tf_op jit(solution)/shard_map/dot_general | solution.py:29
  39.6 1.0 %copy-done = f32[1024,256]{0,1:T(8,128)} copy-done((f32[1024,256]{0,1:T(8,128)}, f32[1024,256]{0,1:T(8,128)S(1)}, u32[]{:S(2)}) %copy-start) | copy-done | bytes 1048600
  41.5 0.8 reduce.1
  42.2 0.7 reshape.133
  42.9 3.2 %all-to-all-start.2 = ((f32[4,1,256]{2,1,0:T(1,128)}), f32[4,1,256]{2,1,0:T(1,128)S(1)}, u32[]{:S(2)}, u32[]{:S(2)}) async-start(f32[4,1,256]{2,1,0:T(1,128)} %reshape.133), calls=%async_computation.2 | async-start | bytes 8192 | tf_op jit(solution)/shard_map/all_to_all | solution.py:87
  46.3 0.8 reduce.3
  47.1 0.7 reshape.131
  47.8 2.2 %all-to-all-done.2 = f32[4,1,256]{2,1,0:T(1,128)S(1)} async-done(((f32[4,1,256]{2,1,0:T(1,128)}), f32[4,1,256]{2,1,0:T(1,128)S(1)}, u32[]{:S(2)}, u32[]{:S(2)}) %all-to-all-start.2) | async-done | bytes 4128 | tf_op jit(solution)/shard_map/all_to_all | solution.py:87
  49.9 3.3 %all-to-all-start.1 = ((f32[4,1,256]{2,1,0:T(1,128)}), f32[4,1,256]{2,1,0:T(1,128)S(1)}, u32[]{:S(2)}, u32[]{:S(2)}) async-start(f32[4,1,256]{2,1,0:T(1,128)} %reshape.131), calls=%async_computation.1 | async-start | bytes 8192 | tf_op jit(solution)/shard_map/all_to_all | solution.py:86
  53.2 1.8 %multiply_add_fusion = f32[1024,512]{1,0:T(8,128)S(1)} fusion(f32[1024,512]{1,0:T(8,128)S(1)} %get-tuple-element.318, bf16[256,512]{1,0:T(8,128)(2,1)S(1)} %get-tuple-element.320, f32[1024]{0:T(1024)S(1)} %get-tuple-element.393, f32[1024,256]{0,1:T(8,128)} %copy-done, pred[32,8,8,128]{3,2,1,0:T(8,128)(4,1)S(1)} %bitcast.101, f32[1024]{0:T(1024)S(1)} %max.13), kind=kOutput, calls=%fused_computation.23 | convolution fusion | flops 270270464 | bytes 5775360 | tf_op jit(solution)/shard_map/dot_general | solution.py:38
  55.0 2.6 %copy.29 = f32[1,8,128,512]{3,1,0,2:T(8,128)} copy(f32[1,8,128,512]{3,2,1,0:T(8,128)S(1)} %bitcast.98) | data formatting | bytes 4194304 | tf_op jit(solution)/shard_map/broadcast_in_dim;reshape | solution.py:88
  57.6 3.6 %all-to-all-start = ((f32[1,8,128,512]{3,1,0,2:T(8,128)}), f32[1,8,128,512]{3,1,0,2:T(8,128)S(1)}, u32[]{:S(2)}, u32[]{:S(2)}) async-start(f32[1,8,128,512]{3,1,0,2:T(8,128)} %copy.29), calls=%async_computation | async-start | bytes 4194304 | tf_op jit(solution)/shard_map/all_to_all | solution.py:88
  61.2 0.6 reduce.2
  62.0 0.6 reduce.4
  63.0 23.8 %all-to-all-done = f32[1,8,128,512]{3,1,0,2:T(8,128)S(1)} async-done(((f32[1,8,128,512]{3,1,0,2:T(8,128)}), f32[1,8,128,512]{3,1,0,2:T(8,128)S(1)}, u32[]{:S(2)}, u32[]{:S(2)}) %all-to-all-start) | async-done | bytes 2097184 | tf_op jit(solution)/shard_map/all_to_all | solution.py:88
  86.8 1.2 %fusion.13 = f32[8,32,512]{2,1,0:T(8,128)S(1)} fusion(f32[1,8,4,32,512]{4,1,3,2,0:T(8,128)S(1)} %bitcast.97, f32[4,8,32]{2,0,1:T(4,128)S(1)} %get-tuple-element.391), kind=kLoop, calls=%fused_computation.22 | loop fusion | flops 917504 | bytes 2625536 | tf_op jit(solution)/shard_map/reduce_sum | solution.py:92
  88.1 2.9 %fusion.17 = bf16[8,32,128]{2,0,1:T(8,128)(2,1)S(1)} fusion(bf16[32,512,128]{2,1,0:T(8,128)(2,1)} %param.15, bf16[8,32,512]{2,1,0:T(8,128)(2,1)S(1)} %divide_convert_fusion), kind=kOutput, calls=%fused_computation.29 | convolution fusion | flops 33587200 | bytes 4521984 | tf_op jit(solution)/shard_map/qhl,hld->qhd/dot_general | solution.py:95
  91.0 0.7 copy.36
  (56 shorter events, 6.3 us)
Async XLA Ops:
  5.7 12.1 %collective-permute-start = (bf16[256,512]{1,0:T(8,128)(2,1)S(1)}, bf16[256,512]{1,0:T(8,128)(2,1)S(1)}, u32[]{:S(2)}, u32[]{:S(2)}) collective-permute-start(bf16[256,512]{1,0:T(8,128)(2,1)S(1)} %copy.69), channel_id=1, source_target_pairs={{0,4},{4,8},{8,12},{12,0},{1,5},{5,9},{9,13},{13,1},{2,6},{6,10},{... | collective-permute-start | bytes 786440 | tf_op jit(solution)/shard_map/while/body/eval_jaxpr/ppermute | solution.py:14
  8.8 9.0 %collective-permute-start.1 = (bf16[64,256]{1,0:T(8,128)(2,1)S(1)}, bf16[64,256]{1,0:T(8,128)(2,1)S(1)}, u32[]{:S(2)}, u32[]{:S(2)}) collective-permute-start(bf16[64,256]{1,0:T(8,128)(2,1)S(1)} %copy.70), channel_id=1, source_target_pairs={{0,4},{4,8},{8,12},{12,0},{1,5},{5,9},{9,13},{13,1},{2,6},{6,10},{... | collective-permute-start | bytes 98312 | tf_op jit(solution)/shard_map/while/body/eval_jaxpr/ppermute | solution.py:14
  17.9 10.0 %collective-permute-start = (bf16[256,512]{1,0:T(8,128)(2,1)S(1)}, bf16[256,512]{1,0:T(8,128)(2,1)S(1)}, u32[]{:S(2)}, u32[]{:S(2)}) collective-permute-start(bf16[256,512]{1,0:T(8,128)(2,1)S(1)} %copy.69), channel_id=1, source_target_pairs={{0,4},{4,8},{8,12},{12,0},{1,5},{5,9},{9,13},{13,1},{2,6},{6,10},{... | collective-permute-start | bytes 786440 | tf_op jit(solution)/shard_map/while/body/eval_jaxpr/ppermute | solution.py:14
  18.5 9.4 %collective-permute-start.1 = (bf16[64,256]{1,0:T(8,128)(2,1)S(1)}, bf16[64,256]{1,0:T(8,128)(2,1)S(1)}, u32[]{:S(2)}, u32[]{:S(2)}) collective-permute-start(bf16[64,256]{1,0:T(8,128)(2,1)S(1)} %copy.70), channel_id=1, source_target_pairs={{0,4},{4,8},{8,12},{12,0},{1,5},{5,9},{9,13},{13,1},{2,6},{6,10},{... | collective-permute-start | bytes 98312 | tf_op jit(solution)/shard_map/while/body/eval_jaxpr/ppermute | solution.py:14
  27.9 9.2 %collective-permute-start = (bf16[256,512]{1,0:T(8,128)(2,1)S(1)}, bf16[256,512]{1,0:T(8,128)(2,1)S(1)}, u32[]{:S(2)}, u32[]{:S(2)}) collective-permute-start(bf16[256,512]{1,0:T(8,128)(2,1)S(1)} %copy.69), channel_id=1, source_target_pairs={{0,4},{4,8},{8,12},{12,0},{1,5},{5,9},{9,13},{13,1},{2,6},{6,10},{... | collective-permute-start | bytes 786440 | tf_op jit(solution)/shard_map/while/body/eval_jaxpr/ppermute | solution.py:14
  28.0 9.1 %collective-permute-start.1 = (bf16[64,256]{1,0:T(8,128)(2,1)S(1)}, bf16[64,256]{1,0:T(8,128)(2,1)S(1)}, u32[]{:S(2)}, u32[]{:S(2)}) collective-permute-start(bf16[64,256]{1,0:T(8,128)(2,1)S(1)} %copy.70), channel_id=1, source_target_pairs={{0,4},{4,8},{8,12},{12,0},{1,5},{5,9},{9,13},{13,1},{2,6},{6,10},{... | collective-permute-start | bytes 98312 | tf_op jit(solution)/shard_map/while/body/eval_jaxpr/ppermute | solution.py:14
  39.5 1.0 %copy-start = (f32[1024,256]{0,1:T(8,128)}, f32[1024,256]{0,1:T(8,128)S(1)}, u32[]{:S(2)}) copy-start(f32[1024,256]{0,1:T(8,128)S(1)} %get-tuple-element.397) | copy-start | bytes 3145732
  42.9 7.0 %all-to-all-start.2 = ((f32[4,1,256]{2,1,0:T(1,128)}), f32[4,1,256]{2,1,0:T(1,128)S(1)}, u32[]{:S(2)}, u32[]{:S(2)}) async-start(f32[4,1,256]{2,1,0:T(1,128)} %reshape.133), calls=%async_computation.2 | async-start | bytes 8192 | tf_op jit(solution)/shard_map/all_to_all | solution.py:87
  49.9 7.6 %all-to-all-start.1 = ((f32[4,1,256]{2,1,0:T(1,128)}), f32[4,1,256]{2,1,0:T(1,128)S(1)}, u32[]{:S(2)}, u32[]{:S(2)}) async-start(f32[4,1,256]{2,1,0:T(1,128)} %reshape.131), calls=%async_computation.1 | async-start | bytes 8192 | tf_op jit(solution)/shard_map/all_to_all | solution.py:86
  57.6 29.2 %all-to-all-start = ((f32[1,8,128,512]{3,1,0,2:T(8,128)}), f32[1,8,128,512]{3,1,0,2:T(8,128)S(1)}, u32[]{:S(2)}, u32[]{:S(2)}) async-start(f32[1,8,128,512]{3,1,0,2:T(8,128)} %copy.29), calls=%async_computation | async-start | bytes 4194304 | tf_op jit(solution)/shard_map/all_to_all | solution.py:88
where the time goes:
time: 92.4 us; the launch traced here: 91.6 us
  waiting for transfers between devices  30.7 us (33%)
  starting transfers between devices  17.6 us (19%)
  other arithmetic  16 us (17%)
  matrix products  15.3 us (17%)
  local copies, waits for them, and re-layouts  11.6 us (13%)
    all_to_all x1, waiting for transfers between devices, shards(): lax.all_to_all(running_out[None], ('sect', 'sub'), split_axis=2, concat_a...  23.8 us
    ppermute x6, starting transfers between devices, shifted(): return lax.ppermute(value, axis, pairs)  7.47 us
    dot_general x4, matrix products, absorb_block(): lax.dot_general(latent_rows, block_latent, (((1,), (1,)), ((), ())), pref...  6.76 us
    reduce_sum x4, other arithmetic, absorb(): length = jnp.sum(jnp.where(block_ids == root, lengths, 0))  5.27 us
    unnamed x9, local copies, waits for them, and re-layouts  4.91 us
    ppermute x6, waiting for transfers between devices, shifted(): return lax.ppermute(value, axis, pairs)  4.64 us
    dot_general x4, matrix products, absorb_block(): jnp.dot(weights.astype(jnp.bfloat16), block_latent, preferred_element_typ...  3.97 us
    all_to_all x1, starting transfers between devices, shards(): lax.all_to_all(running_out[None], ('sect', 'sub'), split_axis=2, concat_a...  3.61 us
  transfers between devices with their start and end apart: 9, of which 5 were waited for; matrix products, arithmetic and copies ran while one was open for 29% of the time, Pallas kernels for 0%

commit v1 on v0

v1 whole, which is shorter than its diff:
```python
import functools
import math

import jax
import jax.numpy as jnp
from jax import lax
from jax.experimental import pallas as pl
from jax.experimental.pallas import tpu as pltpu
from jax.sharding import PartitionSpec as P

lowest_score = -1e30
LANES = 128
MESH = pl.DeviceIdType.MESH


def spread(column, width):
    return jnp.concatenate([column] * (width // LANES), axis=1)


def kernel(
    sizes, query_hbm, rope_q_ref, latent_hbm, rope_hbm, length_ref, position_ref, weight_hbm,
    out_ref,
    query_buf, rope_q_buf, latent_buf, rope_buf, weight_buf, place_buf,
    top_buf, sum_buf, acc_buf, send_buf, send_stat, recv_buf, recv_stat,
    local_sem, z_send, z_recv, pair_send, pair_recv, part_send, part_recv,
):
    blk_count, sect_count, sub_count, chunk_heads = sizes
    query_count, head_count, latent_width = query_hbm.shape
    rope_width = rope_q_ref.shape[1]
    token_count = latent_hbm.shape[1]
    own_heads = head_count // (sect_count * sub_count)
    group_rows = query_count * own_heads
    chunk_count = own_heads // chunk_heads
    chunk_rows = query_count * chunk_heads
    score_scale = 1.0 / math.sqrt(latent_width + rope_width)
    half = token_count // 2
    z = lax.axis_index("blk")
    x = lax.axis_index("sect")
    s = lax.axis_index("sub")

    barrier = pltpu.get_barrier_semaphore()

    def greet(device_id):
        pl.semaphore_signal(barrier, inc=1, device_id=device_id, device_id_type=MESH)

    for step in range(1, sub_count):
        greet({"sub": lax.rem(s + step, sub_count)})
    for step in range(1, sect_count):
        greet({"sect": lax.rem(x + step, sect_count)})

    @pl.when(z > 0)
    def _():
        greet({"blk": z - 1})

    @pl.when(z < blk_count - 1)
    def _():
        greet({"blk": z + 1})

    own_copies = [
        pltpu.make_async_copy(latent_hbm.at[0], latent_buf.at[z, s], local_sem.at[0]),
        pltpu.make_async_copy(rope_hbm.at[0], rope_buf.at[z, s], local_sem.at[1]),
    ]
    query_copies = [
        pltpu.make_async_copy(
            query_hbm.at[:, pl.ds(pl.multiple_of((g * sub_count + s) * own_heads, own_heads), own_heads), :],
            query_buf.at[g], local_sem.at[3 + g],
        )
        for g in range(sect_count)
    ]
    weight_copy = pltpu.make_async_copy(weight_hbm, weight_buf, local_sem.at[2])
    for copy in own_copies + query_copies:
        copy.start()

    neighbours = jnp.where(z > 0, 1, 0) + jnp.where(z < blk_count - 1, 1, 0)
    pl.semaphore_wait(barrier, sub_count - 1 + sect_count - 1 + neighbours)

    def piece(ref_pair, index):
        latent_ref, rope_ref = ref_pair
        if index == 0:
            return rope_ref
        return latent_ref.at[pl.ds((index - 1) * half, half)]

    def held(j, place):
        return latent_buf.at[j, place], rope_buf.at[j, place]

    def z_copy(source, j, index, way, target):
        return pltpu.make_async_remote_copy(
            src_ref=piece(source, index), dst_ref=piece(held(j, s), index),
            send_sem=z_send.at[way, j, index], recv_sem=z_recv.at[j, index],
            device_id={"blk": target}, device_id_type=MESH,
        )

    def pair_copy(source, j, index, step):
        return pltpu.make_async_remote_copy(
            src_ref=piece(source, index), dst_ref=piece(held(j, s), index),
            send_sem=pair_send.at[step - 1, j, index], recv_sem=pair_recv.at[step - 1, j, index],
            device_id={"sub": lax.rem(s + step, sub_count)}, device_id_type=MESH,
        )

    own = (latent_hbm.at[0], rope_hbm.at[0])
    pieces = range(3)
    for index in pieces:
        @pl.when(z < blk_count - 1)
        def _():
            z_copy(own, z, index, 0, z + 1).start()

        @pl.when(z > 0)
        def _():
            z_copy(own, z, index, 1, z - 1).start()

    for index in pieces:
        for step in range(1, sub_count):
            pair_copy(own, z, index, step).start()
    weight_copy.start()

    for q in range(query_count):
        turned = jnp.transpose(rope_q_ref[q].astype(jnp.float32)).astype(jnp.bfloat16)
        rope_q_buf[q] = turned
        place_buf[pl.ds(q * own_heads, own_heads), :] = jnp.full(
            (own_heads, token_count), position_ref[q], jnp.int32
        )
    top_buf[...] = jnp.full(top_buf.shape, lowest_score, jnp.float32)
    sum_buf[...] = jnp.zeros(sum_buf.shape, jnp.float32)
    acc_buf[...] = jnp.zeros(acc_buf.shape, jnp.float32)
    for copy in own_copies + query_copies:
        copy.wait()

    def absorb(j, place, g):
        root = (j * sect_count + x) * sub_count + place
        length = length_ref[root]
        block = latent_buf[j, place]
        heads_at = pl.multiple_of((g * sub_count + s) * own_heads, own_heads)
        rope_rows = rope_q_buf[:, pl.ds(heads_at, own_heads), :].reshape(group_rows, rope_width)
        scores = lax.dot_general(
            query_buf[g].reshape(group_rows, latent_width), block,
            (((1,), (1,)), ((), ())), preferred_element_type=jnp.float32,
        )
        scores = scores + jnp.dot(rope_rows, rope_buf[j, place], preferred_element_type=jnp.float32)
        offsets = lax.broadcasted_iota(jnp.int32, (group_rows, token_count), 1)
        visible = offsets < jnp.minimum(length, place_buf[...] - (root * token_count - 1))
        scores = jnp.where(visible, scores * score_scale, lowest_score)
        old_top = top_buf[g]
        new_top = jnp.maximum(old_top, jnp.max(scores, axis=1, keepdims=True))
        factor = jnp.exp(old_top - new_top)
        weights = jnp.where(visible, jnp.exp(scores - spread(new_top, token_count)), 0.0)
        sum_buf[g] = sum_buf[g] * factor + jnp.sum(weights, axis=1, keepdims=True)
        top_buf[g] = new_top
        acc_buf[g] = acc_buf[g] * spread(factor, latent_width) + jnp.dot(
            weights.astype(jnp.bfloat16), block, preferred_element_type=jnp.float32
        )

    def wait_pair(j, step):
        for index in pieces:
            pair_copy(held(j, s), j, index, step).wait_recv()

    def source_of(step):
        return lax.rem(s + sub_count - step, sub_count)

    def absorb_all(j):
        def over_groups(place):
            def one(g, carry):
                absorb(j, place, g)
                return carry
            lax.fori_loop(0, sect_count, one, 0)

        over_groups(s)
        for step in range(1, sub_count):
            wait_pair(j, step)
            over_groups(source_of(step))

    def pass_on(k):
        for index in pieces:
            for way in range(2):
                j = z - k if way == 0 else z + k
                target = z + 1 if way == 0 else z - 1
                here = j >= 0 if way == 0 else j < blk_count
                further = target < blk_count if way == 0 else target >= 0

                @pl.when(here)
                def _():
                    z_copy(held(j, s), j, index, way, z).wait_recv()

                    @pl.when(further)
                    def _():
                        z_copy(held(j, s), j, index, way, target).start()

                    for step in range(1, sub_count):
                        pair_copy(held(j, s), j, index, step).start()

    absorb_all(z)

    def one_step(k, carry):
        pass_on(k)

        def one_way(way, inner):
            j = z + (2 * way - 1) * k

            @pl.when((j >= 0) & (j < blk_count))
            def _():
                absorb_all(j)
            return inner
        lax.fori_loop(0, 2, one_way, 0)
        return carry

    lax.fori_loop(1, blk_count - 1, one_step, 0)

    if blk_count > 1:
        pass_on(blk_count - 1)
    at_end = ((z == 0) | (z == blk_count - 1)) & (blk_count > 1)
    last = jnp.where(z == 0, blk_count - 1, 0)

    def part_copies(step, c):
        target = {"sect": lax.rem(x + step, sect_count)}
        return [
            pltpu.make_async_remote_copy(
                src_ref=source.at[step - 1, c], dst_ref=landing.at[step - 1, c],
                send_sem=part_send.at[step - 1, c, i], recv_sem=part_recv.at[step - 1, c, i],
                device_id=target, device_id_type=MESH,
            )
            for i, (source, landing) in enumerate(((send_buf, recv_buf), (send_stat, recv_stat)))
        ]

    def rows_of(value, c):
        width = value.shape[-1]
        cut = value.reshape(query_count, own_heads, width)[:, c * chunk_heads:(c + 1) * chunk_heads, :]
        return cut.reshape(chunk_rows, width)

    for step in range(1, sect_count):
        g = lax.rem(x + step, sect_count)

        @pl.when(at_end)
        def _():
            absorb(last, s, g)
            for pair_step in range(1, sub_count):
                if step == 1:
                    wait_pair(last, pair_step)
                absorb(last, source_of(pair_step), g)

        for c in range(chunk_count):
            send_buf[step - 1, c] = rows_of(acc_buf[g], c).astype(jnp.bfloat16)
            send_stat[step - 1, c, 0:8] = jnp.transpose(rows_of(top_buf[g], c))[0:8]
            send_stat[step - 1, c, 8:16] = jnp.transpose(rows_of(sum_buf[g], c))[0:8]
            for copy in part_copies(step, c):
                copy.start()

    @pl.when(at_end)
    def _():
        absorb(last, s, x)
        for pair_step in range(1, sub_count):
            if sect_count == 1:
                wait_pair(last, pair_step)
            absorb(last, source_of(pair_step), x)

    weight_copy.wait()
    row_head = lax.rem(lax.broadcasted_iota(jnp.int32, (chunk_rows, weight_hbm.shape[2]), 0), chunk_heads)
    value_width = weight_hbm.shape[2]
    for c in range(chunk_count):
        tops = [rows_of(top_buf[x], c)]
        sums = [rows_of(sum_buf[x], c)]
        outs = [rows_of(acc_buf[x], c)]
        for step in range(1, sect_count):
            for copy in part_copies(step, c):
                copy.wait_recv()
            stat = recv_stat[step - 1, c]
            tops.append(jnp.transpose(jnp.broadcast_to(stat[0:1], (LANES, chunk_rows))))
            sums.append(jnp.transpose(jnp.broadcast_to(stat[8:9], (LANES, chunk_rows))))
            outs.append(recv_buf[step - 1, c].astype(jnp.float32))
        overall = functools.reduce(jnp.maximum, tops)
        factors = [jnp.exp(top - overall) for top in tops]
        total = sum(part * factor for part, factor in zip(sums, factors))
        latent = sum(
            part * spread(factor / total, latent_width) for part, factor in zip(outs, factors)
        ).astype(jnp.bfloat16)
        result = jnp.zeros((chunk_rows, value_width), jnp.float32)
        for h in range(0, chunk_heads, 2):
            pair = jnp.concatenate(
                [weight_buf[c * chunk_heads + h], weight_buf[c * chunk_heads + h + 1]], axis=1
            )
            both = jnp.dot(latent, pair, preferred_element_type=jnp.float32)
            result = jnp.where(row_head == h, both[:, :value_width], result)
            result = jnp.where(row_head == h + 1, both[:, value_width:], result)
        out_ref[:, c * chunk_heads:(c + 1) * chunk_heads, :] = result.reshape(
            query_count, chunk_heads, value_width
        ).astype(out_ref.dtype)

    for step in range(1, sect_count):
        for c in range(chunk_count):
            for copy in part_copies(step, c):
                copy.wait_send()

    def drain(j, carry):
        for index in pieces:
            @pl.when((j <= z) & (z < blk_count - 1))
            def _():
                z_copy(held(j, s), j, index, 0, z).wait_send()

            @pl.when((j >= z) & (z > 0))
            def _():
                z_copy(held(j, s), j, index, 1, z).wait_send()

            for step in range(1, sub_count):
                pair_copy(held(j, s), j, index, step).wait_send()
        return carry

    lax.fori_loop(0, blk_count, drain, 0)


def shards(query_latent, query_rope, cache_latent, cache_rope, lengths, positions, value_weight):
    query_count, head_count, latent_width = query_latent.shape
    rope_width = query_rope.shape[1]
    token_count = cache_latent.shape[1]
    blk_count, sect_count, sub_count = (lax.axis_size(name) for name in ("blk", "sect", "sub"))
    own_heads, _, value_width = value_weight.shape
    chunk_heads = min(16, own_heads)
    chunk_count = own_heads // chunk_heads
    chunk_rows = query_count * chunk_heads
    group_rows = query_count * own_heads
    peers = max(sect_count - 1, 1)
    pairs = max(sub_count - 1, 1)
    bf16, f32 = jnp.bfloat16, jnp.float32
    anywhere = pl.BlockSpec(memory_space=pl.ANY)
    vmem = pl.BlockSpec(memory_space=pltpu.VMEM)
    smem = pl.BlockSpec(memory_space=pltpu.SMEM)
    dma = pltpu.SemaphoreType.DMA
    return pl.pallas_call(
        functools.partial(kernel, (blk_count, sect_count, sub_count, chunk_heads)),
        out_shape=jax.ShapeDtypeStruct((query_count, own_heads, value_width), bf16),
        in_specs=[anywhere, vmem, anywhere, anywhere, smem, smem, anywhere],
        out_specs=vmem,
        scratch_shapes=[
            pltpu.VMEM((sect_count, query_count, own_heads, latent_width), bf16),
            pltpu.VMEM((query_count, head_count, rope_width), bf16),
            pltpu.VMEM((blk_count, sub_count, token_count, latent_width), bf16),
            pltpu.VMEM((blk_count, sub_count, rope_width, token_count), bf16),
            pltpu.VMEM((own_heads, latent_width, value_width), bf16),
            pltpu.VMEM((group_rows, token_count), jnp.int32),
            pltpu.VMEM((sect_count, group_rows, LANES), f32),
            pltpu.VMEM((sect_count, group_rows, LANES), f32),
            pltpu.VMEM((sect_count, group_rows, latent_width), f32),
            pltpu.VMEM((peers, chunk_count, chunk_rows, latent_width), bf16),
            pltpu.VMEM((peers, chunk_count, 16, chunk_rows), f32),
            pltpu.VMEM((peers, chunk_count, chunk_rows, latent_width), bf16),
            pltpu.VMEM((peers, chunk_count, 16, chunk_rows), f32),
            dma((3 + sect_count,)),
            dma((2, blk_count, 3)),
            dma((blk_count, 3)),
            dma((pairs, blk_count, 3)),
            dma((pairs, blk_count, 3)),
            dma((peers, chunk_count, 2)),
            dma((peers, chunk_count, 2)),
        ],
        compiler_params=pltpu.CompilerParams(
            collective_id=0, has_side_effects=True, vmem_limit_bytes=60 * 1024 * 1024
        ),
    )(query_latent, query_rope, cache_latent, cache_rope, lengths, positions, value_weight)


def solution(mesh):
    placed = (
        P(("rep", "blk"), None, None),
        P(("rep", "blk"), None, None),
        P(("rep", "blk", "sect", "sub"), None, None),
        P(("rep", "blk", "sect", "sub"), None, None),
        P("rep"),
        P(("rep", "blk")),
        P(("sect", "sub"), None, None),
    )
    return jax.shard_map(
        shards,
        mesh=mesh,
        in_specs=placed,
        out_specs=P(("rep", "blk"), ("sect", "sub"), None),
        check_vma=False,
    )
```

time: 92.4 us -> 39 us (0.42)
  Pallas kernels: 0 us -> 37.4 us
  waiting for transfers between devices: 30.7 us -> 0 us
  starting transfers between devices: 17.6 us -> 0 us
  other arithmetic: 16 us -> 0 us
  matrix products: 15.3 us -> 0 us
  local copies, waits for them, and re-layouts: 11.6 us -> 1.47 us
    pallas_call x0 -> x1, Pallas kernels: none -> 37.4 us  [shards(): pl.pallas_call(functools.partial(kernel, (blk_count, sect_count, sub_coun...]
    all_to_all x3 -> x0, waiting for transfers between devices: 26 us -> none  [the longest x1 23.8 us: shards(): lax.all_to_all(running_out[None], ('sect', 'sub'), split_axis=2, concat_a...]
    dot_general x13 -> x0, matrix products: 15.3 us -> none  [the longest x4 6.76 us: absorb_block(): lax.dot_general(latent_rows, block_latent, (((1,), (1,)), ((), ())), pref...]
    all_to_all x3 -> x0, starting transfers between devices: 10.1 us -> none  [the longest x1 3.61 us: shards(): lax.all_to_all(running_out[None], ('sect', 'sub'), split_axis=2, concat_a...]
    reduce_sum x10 -> x0, other arithmetic: 7.56 us -> none  [the longest x4 5.27 us: absorb(): length = jnp.sum(jnp.where(block_ids == root, lengths, 0))]
    ppermute x6 -> x0, starting transfers between devices: 7.47 us -> none  [shifted(): return lax.ppermute(value, axis, pairs)]
    ppermute x6 -> x0, waiting for transfers between devices: 4.64 us -> none  [shifted(): return lax.ppermute(value, axis, pairs)]
    unnamed x9 -> x1, local copies, waits for them, and re-layouts: 4.91 us -> 1.47 us
  transfers between devices with their start and end apart: 9 -> 0, of which waited for: 5 -> 0; matrix products, arithmetic and copies ran while one was open for 29% -> 0% of each run, Pallas kernels for 0% -> 0%
where the time goes in v1:
time: 39 us; the launch traced here: 38.8 us
  Pallas kernels  37.4 us (96%)
  local copies, waits for them, and re-layouts  1.47 us (4%)
    pallas_call x1, Pallas kernels, shards(): pl.pallas_call(functools.partial(kernel, (blk_count, sect_count, sub_coun...  37.4 us
    unnamed x1, local copies, waits for them, and re-layouts  1.47 us

profile of v1, /device:TPU:0, one launch (start us, length us, event | category | flops | bytes accessed | tf_op | source)
XLA Modules:
  0.0 38.8 jit_solution(1748412107994598648)
XLA Ops:
  0.0 37.4 %shard_map.73 = bf16[8,32,128]{2,1,0:T(8,128)(2,1)} custom-call(bf16[8,128,512]{2,1,0:T(8,128)(2,1)} %query_hbm.1, bf16[8,64,128]{2,1,0:T(8,128)(2,1)} %rope_q_ref.1, bf16[1,256,512]{2,1,0:T(8,128)(2,1)} %latent_hbm.1, bf16[1,64,256]{2,1,0:T(8,128)(2,1)} %rope_hbm.1, s32[16]{0:T(128)} %length_ref.1, s32[8]{0:T(128)} %position_ref.1, ...), custom_call_target="tpu_custom_call" | custom-call | tf_op jit(solution)/shard_map/pallas_call | solution.py:325
  37.4 1.5 %copy.9 = bf16[8,32,128]{2,1,0:T(8,128)(2,1)} copy(bf16[8,32,128]{2,1,0:T(8,128)(2,1)} %shard_map.73) | data formatting | bytes 131072

commit v2 on v1

--- a/solution.py
+++ b/solution.py
@@ -18,15 +18,15 @@
 
 
 def kernel(
-    sizes, query_hbm, rope_q_ref, latent_hbm, rope_hbm, length_ref, position_ref, weight_hbm,
+    sizes, query_hbm, rope_q_hbm, latent_hbm, rope_hbm, length_hbm, position_hbm, weight_hbm,
     out_ref,
-    query_buf, rope_q_buf, latent_buf, rope_buf, weight_buf, place_buf,
+    rope_q_ref, length_ref, position_ref, query_buf, rope_q_buf, latent_buf, rope_buf, weight_buf, place_buf,
     top_buf, sum_buf, acc_buf, send_buf, send_stat, recv_buf, recv_stat,
     local_sem, z_send, z_recv, pair_send, pair_recv, part_send, part_recv,
 ):
     blk_count, sect_count, sub_count, chunk_heads = sizes
     query_count, head_count, latent_width = query_hbm.shape
-    rope_width = rope_q_ref.shape[1]
+    rope_width = rope_q_hbm.shape[1]
     token_count = latent_hbm.shape[1]
     own_heads = head_count // (sect_count * sub_count)
     group_rows = query_count * own_heads
@@ -68,7 +68,13 @@
         for g in range(sect_count)
     ]
     weight_copy = pltpu.make_async_copy(weight_hbm, weight_buf, local_sem.at[2])
-    for copy in own_copies + query_copies:
+    small_copies = [
+        pltpu.make_async_copy(source, landing, local_sem.at[3 + sect_count + i])
+        for i, (source, landing) in enumerate(
+            ((rope_q_hbm, rope_q_ref), (length_hbm, length_ref), (position_hbm, position_ref))
+        )
+    ]
+    for copy in small_copies + own_copies + query_copies:
         copy.start()
 
     neighbours = jnp.where(z > 0, 1, 0) + jnp.where(z < blk_count - 1, 1, 0)
@@ -113,6 +119,8 @@
             pair_copy(own, z, index, step).start()
     weight_copy.start()
 
+    for copy in small_copies:
+        copy.wait()
     for q in range(query_count):
         turned = jnp.transpose(rope_q_ref[q].astype(jnp.float32)).astype(jnp.bfloat16)
         rope_q_buf[q] = turned
@@ -318,16 +326,18 @@
     peers = max(sect_count - 1, 1)
     pairs = max(sub_count - 1, 1)
     bf16, f32 = jnp.bfloat16, jnp.float32
-    anywhere = pl.BlockSpec(memory_space=pl.ANY)
+    hbm = pl.BlockSpec(memory_space=pltpu.HBM)
     vmem = pl.BlockSpec(memory_space=pltpu.VMEM)
-    smem = pl.BlockSpec(memory_space=pltpu.SMEM)
     dma = pltpu.SemaphoreType.DMA
     return pl.pallas_call(
         functools.partial(kernel, (blk_count, sect_count, sub_count, chunk_heads)),
         out_shape=jax.ShapeDtypeStruct((query_count, own_heads, value_width), bf16),
-        in_specs=[anywhere, vmem, anywhere, anywhere, smem, smem, anywhere],
+        in_specs=[hbm] * 7,
         out_specs=vmem,
         scratch_shapes=[
+            pltpu.VMEM(query_rope.shape, bf16),
+            pltpu.SMEM(lengths.shape, jnp.int32),
+            pltpu.SMEM(positions.shape, jnp.int32),
             pltpu.VMEM((sect_count, query_count, own_heads, latent_width), bf16),
             pltpu.VMEM((query_count, head_count, rope_width), bf16),
             pltpu.VMEM((blk_count, sub_count, token_count, latent_width), bf16),
@@ -341,7 +351,7 @@
             pltpu.VMEM((peers, chunk_count, 16, chunk_rows), f32),
             pltpu.VMEM((peers, chunk_count, chunk_rows, latent_width), bf16),
             pltpu.VMEM((peers, chunk_count, 16, chunk_rows), f32),
-            dma((3 + sect_count,)),
+            dma((6 + sect_count,)),
             dma((2, blk_count, 3)),
             dma((blk_count, 3)),
             dma((pairs, blk_count, 3)),

time: 39 us -> 38.1 us (0.977)
  Pallas kernels: 37.4 us -> 36.4 us
    pallas_call x1, Pallas kernels: 37.4 us -> 36.4 us  [shards(): pl.pallas_call(functools.partial(kernel, (blk_count, sect_count, sub_coun...]
where the time goes in v2:
time: 38.1 us; the launch traced here: 37.9 us
  Pallas kernels  36.4 us (96%)
  local copies, waits for them, and re-layouts  1.47 us (4%)
    pallas_call x1, Pallas kernels, shards(): pl.pallas_call(functools.partial(kernel, (blk_count, sect_count, sub_coun...  36.4 us
    unnamed x1, local copies, waits for them, and re-layouts  1.47 us

profile of v2, /device:TPU:0, one launch (start us, length us, event | category | flops | bytes accessed | tf_op | source)
XLA Modules:
  0.0 37.9 jit_solution(4258809779918418258)
XLA Ops:
  0.0 36.4 %shard_map.73 = bf16[8,32,128]{2,1,0:T(8,128)(2,1)} custom-call(bf16[8,128,512]{2,1,0:T(8,128)(2,1)} %query_hbm.1, bf16[8,64,128]{2,1,0:T(8,128)(2,1)} %rope_q_hbm.1, bf16[1,256,512]{2,1,0:T(8,128)(2,1)} %latent_hbm.1, bf16[1,64,256]{2,1,0:T(8,128)(2,1)} %rope_hbm.1, s32[16]{0:T(128)} %length_hbm.1, s32[8]{0:T(128)} %position_hbm.1, ...), custom_call_target="tpu_custom_call" | custom-call | tf_op jit(solution)/shard_map/pallas_call | solution.py:332
  36.4 1.5 %copy.9 = bf16[8,32,128]{2,1,0:T(8,128)(2,1)} copy(bf16[8,32,128]{2,1,0:T(8,128)(2,1)} %shard_map.73) | data formatting | bytes 131072
